TPU v7x, 512 devices: a whole 4x8x8 slice. The times are simulated.
512 devices in a mesh: seq: 64 (over x, z, core), rep: 8 (over y).
Axes of the slice: x: 4, y: 8, z: 8, core: 2. Of those that a mesh axis runs over, the one named last changes fastest.
Arguments:
- token_ids: int32 [32, 4], P('rep'), parts along dimension 0, may hold values from 0 to 24703
- cache_lengths: int32 [32], P('rep'), parts along dimension 0, may hold values from 1 to 8192, 8216 in all
- embed_table: bfloat16 [2048, 24704], P('seq'), may hold values from -0.119628906 to 0.119628906
- key_cache: bfloat16 [32, 8192, 512], P('rep', 'seq'), parts along dimension 0, may hold values from -4000 to 4000
- value_cache: bfloat16 [32, 8192, 512], P('rep', 'seq'), parts along dimension 0, may hold values from -24 to 24
- norm_attn: bfloat16 [2048], replicated, may hold values from 0.25 to 1.75
- norm_mlp: bfloat16 [2048], replicated, may hold values from 0.25 to 1.75
- w_qkv: bfloat16 [2048, 3072], P(None, 'seq'), may hold values from -0.125 to 0.125
- w_out: bfloat16 [2048, 2048], P(None, 'seq'), may hold values from -0.125 to 0.125
- w_gate: bfloat16 [2048, 8192], P(None, 'seq'), may hold values from -0.125 to 0.125
- w_up: bfloat16 [2048, 8192], P(None, 'seq'), may hold values from -0.125 to 0.125
- w_down: bfloat16 [8192, 2048], P('seq'), may hold values from -0.0625 to 0.0625
Outputs:
- layer_out: bfloat16 [32, 4, 2048], P('rep'), parts along dimension 0
There are 8 independent parts, one for each index of `rep`. A program takes and returns all parts, laid end to end along the dimension named above; an argument that names none is the same for every part. Nothing has to cross between parts.
All inputs are finite; a program needn't handle non-finite values.
Results may differ from a plain program's by a relative error of at most 0.012.
The roundings to bfloat16 on the way count: a program that leaves them out, or rounds other values in their place, can miss the bound.
Values may be sent and summed in bfloat16 or wider, within the bound.
A program may use at most 128 MiB of HBM per device.

v0:
```python
import jax
import jax.numpy as jnp
from jax import lax
from jax.sharding import PartitionSpec as P

H = 32
KVH = 8
HD = 64
STEPS = 4
norm_epsilon = 1e-05
embed_factor = 12.0
score_factor = 0.015625
branch_factor = 0.22
rope_base = 10000000.0
masked_floor = -1e30


def rms_scale(resid, gain):
    mean_square = jnp.mean(resid * resid, axis=-1, keepdims=True)
    return resid * lax.rsqrt(mean_square + norm_epsilon) * gain.astype(jnp.float32)


def rotate(vectors, where):
    half = vectors.shape[-1] // 2
    freqs = rope_base ** (-2.0 * jnp.arange(half, dtype=jnp.float32) / vectors.shape[-1])
    angle = where[..., None] * freqs
    cosine = jnp.cos(angle)
    sine = jnp.sin(angle)
    first_half = vectors[..., :half]
    second_half = vectors[..., half:]
    return jnp.concatenate(
        [first_half * cosine - second_half * sine, second_half * cosine + first_half * sine],
        axis=-1,
    )


def partial_softmax(queries, keys, values, valid):
    scores = (
        jnp.einsum("rskgd,rpkd->rskgp", queries, keys, preferred_element_type=jnp.float32)
        * score_factor
    )
    maxima = jnp.max(jnp.where(valid, scores, masked_floor), axis=-1)
    expo = jnp.exp(jnp.where(valid, scores - maxima[..., None], masked_floor))
    totals = jnp.sum(expo, axis=-1)
    outputs = jnp.einsum(
        "rskgp,rpkd->rskgd", expo.astype(jnp.bfloat16), values, preferred_element_type=jnp.float32
    )
    return (maxima, totals, outputs)


def shards(
    token_ids,
    cache_lengths,
    embed_table,
    key_cache,
    value_cache,
    norm_attn,
    norm_mlp,
    w_qkv,
    w_out,
    w_gate,
    w_up,
    w_down,
):
    place = lax.axis_index("seq")
    req_all = token_ids.shape[0]
    steps = token_ids.shape[1]
    ctx_own = key_cache.shape[1]
    att_width = H * HD
    kv_width = KVH * HD
    group = H // KVH
    picked = jnp.take(embed_table, token_ids.reshape(-1), axis=1)
    whole = lax.all_gather(picked, "seq", axis=0, tiled=True)
    resid = (
        jnp.transpose(whole, (1, 0)).reshape(req_all, steps, -1).astype(jnp.float32) * embed_factor
    )
    slot_pos = place * ctx_own + jnp.arange(ctx_own, dtype=jnp.int32)
    cache_valid = (slot_pos[None, :] < cache_lengths[:, None]).reshape(req_all, 1, 1, 1, ctx_own)
    cache_keys = key_cache.reshape(req_all, ctx_own, KVH, HD)
    cache_values = value_cache.reshape(req_all, ctx_own, KVH, HD)
    normed = rms_scale(resid, norm_attn).astype(jnp.bfloat16)
    qkv_cols = jnp.einsum("rsd,dc->rsc", normed, w_qkv, preferred_element_type=jnp.float32).astype(
        jnp.bfloat16
    )
    qkv_all = lax.all_gather(qkv_cols, "seq", axis=2, tiled=True)
    where = (cache_lengths[:, None] + jnp.arange(steps, dtype=jnp.int32)[None, :]).astype(
        jnp.float32
    )
    queries = rotate(
        qkv_all[..., :att_width].reshape(req_all, steps, H, HD).astype(jnp.float32),
        where[..., None],
    ).astype(jnp.bfloat16)
    keys_new = rotate(
        qkv_all[..., att_width : att_width + kv_width]
        .reshape(req_all, steps, KVH, HD)
        .astype(jnp.float32),
        where[..., None],
    ).astype(jnp.bfloat16)
    values_new = qkv_all[..., att_width + kv_width :].reshape(req_all, steps, KVH, HD)
    grouped = queries.reshape(req_all, steps, KVH, group, HD)
    cache_max, cache_total, cache_out = partial_softmax(
        grouped, cache_keys, cache_values, cache_valid
    )
    fresh_valid = (
        jnp.arange(steps, dtype=jnp.int32)[None, :] <= jnp.arange(steps, dtype=jnp.int32)[:, None]
    ).reshape(1, steps, 1, 1, steps)
    fresh_max, fresh_total, fresh_out = partial_softmax(grouped, keys_new, values_new, fresh_valid)
    overall = jnp.maximum(lax.pmax(cache_max, "seq"), fresh_max)
    cache_scale = jnp.exp(cache_max - overall)
    packed = jnp.concatenate(
        [cache_scale[..., None] * cache_out, (cache_scale * cache_total)[..., None]], axis=-1
    )
    summed = lax.psum(packed, "seq")
    fresh_scale = jnp.exp(fresh_max - overall)
    numer = summed[..., :HD] + fresh_scale[..., None] * fresh_out
    denom = summed[..., HD] + fresh_scale * fresh_total
    attention = (numer / denom[..., None]).astype(jnp.bfloat16).reshape(req_all, steps, att_width)
    proj_cols = jnp.einsum(
        "rsa,ac->rsc", attention, w_out, preferred_element_type=jnp.float32
    ).astype(jnp.bfloat16)
    projected = lax.all_gather(proj_cols, "seq", axis=2, tiled=True)
    middle = resid + branch_factor * projected.astype(jnp.float32)
    normed_mlp = rms_scale(middle, norm_mlp).astype(jnp.bfloat16)
    gate = jnp.einsum("rsd,df->rsf", normed_mlp, w_gate, preferred_element_type=jnp.float32)
    upward = jnp.einsum("rsd,df->rsf", normed_mlp, w_up, preferred_element_type=jnp.float32)
    hidden = (jax.nn.silu(gate) * upward).astype(jnp.bfloat16)
    down_part = jnp.einsum("rsf,fd->rsd", hidden, w_down, preferred_element_type=jnp.float32)
    down = lax.psum(down_part, "seq")
    return (middle + branch_factor * down).astype(jnp.bfloat16)


def solution(mesh):
    return jax.shard_map(
        shards,
        mesh=mesh,
        in_specs=(
            P("rep", None),
            P("rep"),
            P("seq", None),
            P("rep", "seq", None),
            P("rep", "seq", None),
            P(),
            P(),
            P(None, "seq"),
            P(None, "seq"),
            P(None, "seq"),
            P(None, "seq"),
            P("seq", None),
        ),
        out_specs=P("rep", None, None),
        check_vma=False,
    )
```

profile of v0, /device:TPU:1, one launch (start us, length us, event | category | flops | bytes accessed | tf_op | source)
XLA Modules:
  0.0 811.6 jit_solution(16249509916441426397)
XLA Ops:
  6.5 0.8 reshape.176
  7.4 0.8 reshape.175
  8.2 6.4 copy.89
  14.6 4.2 gather_fusion
  18.9 51.6 %all-gather = bf16[64,32,16]{1,2,0:T(8,128)(2,1)S(1)} all-gather(bf16[1,32,16]{1,2,0:T(8,128)(2,1)S(1)} %select_bitcast_fusion), channel_id=1, replica_groups=mesh['seq'=64,'rep'=8] {'seq'}, dimensions={0}, use_global_device_ids=true | all-gather | bytes 66560 | tf_op jit(solution)/shard_map/all_gather | solution.py:73
  70.4 0.3 copy.90
  70.8 0.2 copy.91
  71.0 0.2 reshape.194
  71.2 0.1 multiply_reduce_fusion.1
  71.4 0.1 mul.209
  71.5 0.2 convolution_convert_fusion.1
  71.7 0.1 copy.92
  71.9 51.1 %all_gather.10 = bf16[4,4,3072]{1,0,2:T(4,128)(2,1)S(1)} all-gather(bf16[4,4,48]{1,0,2:T(4,128)(2,1)S(1)} %copy.92), channel_id=1, replica_groups=mesh['seq'=64,'rep'=8] {'seq'}, dimensions={2}, use_global_device_ids=true | all-gather | bytes 99840 | tf_op jit(solution)/shard_map/all_gather | solution.py:85
  123.0 0.7 slice.38
  123.8 1.2 fusion.44
  124.9 2.2 copy.124
  127.1 1.0 reshape.182
  128.2 0.3 copy.125
  128.5 0.1 reshape.183
  128.6 0.1 fusion.45
  128.8 1.3 copy.96
  130.1 0.1 multiply_cosine_fusion
  130.3 0.1 subtract_convert_fusion
  130.4 0.2 pad_maximum_fusion.1
  130.6 0.4 select_reduce_fusion.1
  131.0 243.2 %pmax.7 = f32[4,4,8,4]{3,1,2,0:T(4,128)S(1)} all-reduce(f32[4,4,8,4]{3,1,2,0:T(4,128)S(1)} %get-tuple-element.19), channel_id=1, replica_groups=mesh['seq'=64,'rep'=8] {'seq'}, use_global_device_ids=true, to_apply=%region_2.3 | all-reduce | flops 512 | bytes 4096 | tf_op jit(solution)/shard_map/pmax | solution.py:108
  374.2 0.4 fusion.16
  374.7 0.3 copy.100
  375.0 1.3 select_reduce_fusion
  376.4 0.9 copy.102
  377.3 0.5 fusion.1
  377.7 0.9 pad_maximum_fusion
  378.7 0.2 all-reduce.5.cloned.1.call-start
  378.9 0.4 fusion.18
  379.3 185.2 %all-reduce.3.cloned.1.call-done = f32[4,4,8,4,65]{4,3,1,2,0:T(4,128)} async-done(((f32[4,4,8,4,65]{4,3,1,2,0:T(4,128)}), f32[4,4,8,4,65]{4,3,1,2,0:T(4,128)}) %all-reduce.3.cloned.1.call-update) | async-done | bytes 133136 | tf_op jit(solution)/shard_map/psum | solution.py:113
  564.5 1.1 slice.46
  565.7 0.9 copy.123
  566.6 1.6 fusion.6
  568.3 0.1 reshape.180
  568.4 0.2 convolution_convert_fusion
  568.6 0.1 copy.109
  568.7 48.3 %all_gather.11 = bf16[4,4,2048]{1,0,2:T(4,128)(2,1)S(1)} all-gather(bf16[4,4,32]{1,0,2:T(4,128)(2,1)S(1)} %copy.109), channel_id=1, replica_groups=mesh['seq'=64,'rep'=8] {'seq'}, dimensions={2}, use_global_device_ids=true | all-gather | bytes 66560 | tf_op jit(solution)/shard_map/all_gather | solution.py:121
  617.0 1.3 copy.110
  618.3 0.1 multiply_reduce_fusion
  618.5 1.3 fusion.12
  619.8 1.1 fusion.8
  620.9 182.2 %all-reduce.5.cloned.1.call-done = f32[4,4,2048]{2,1,0:T(4,128)} async-done(((f32[4,4,2048]{2,1,0:T(4,128)}), f32[4,4,2048]{2,1,0:T(4,128)}) %all-reduce.5.cloned.1.call-update) | async-done | bytes 131088 | tf_op jit(solution)/shard_map/psum | solution.py:128
  803.2 1.6 add_convert_fusion.1
  (39 shorter events, 0.6 us)
Async XLA Ops:
  6.5 613.2 %copy-start = (bf16[128,2048]{1,0:T(8,128)(2,1)S(1)}, bf16[128,2048]{1,0:T(8,128)(2,1)}, u32[]{:S(2)}) copy-start(bf16[128,2048]{1,0:T(8,128)(2,1)} %param.23) | copy-start | bytes 1572868
  6.5 558.0 %all-reduce.3.cloned.1.call-start = ((), (), s32[]{:S(2)}) async-start(), calls=%async_computation | async-start | bytes 524288 | tf_op jit(solution)/shard_map/psum | solution.py:113
  8.1 63.3 %copy-start.4 = (bf16[2048]{0:T(1024)(128)(2,1)S(1)}, bf16[2048]{0:T(1024)(128)(2,1)}, u32[]{:S(2)}) copy-start(bf16[2048]{0:T(1024)(128)(2,1)} %param.17) | copy-start | bytes 12292
  8.1 63.3 %copy-start.7 = (bf16[2048,48]{0,1:T(8,128)(2,1)S(1)}, bf16[2048,48]{0,1:T(8,128)(2,1)}, u32[]{:S(2)}) copy-start(bf16[2048,48]{0,1:T(8,128)(2,1)} %param.19) | copy-start | bytes 589828
  123.8 4.4 copy-start.6
  127.1 247.6 %copy-start.1 = (bf16[4,128,512]{2,1,0:T(8,128)(2,1)S(1)}, bf16[4,128,512]{2,1,0:T(8,128)(2,1)}, u32[]{:S(2)}) copy-start(bf16[4,128,512]{2,1,0:T(8,128)(2,1)} %param.16) | copy-start | bytes 1572868
  376.3 3.0 copy-start.5
  377.3 189.3 %copy-start.3 = (bf16[4,4,512]{1,0,2:T(4,128)(2,1)S(1)}, bf16[4,4,512]{1,0,2:T(4,128)(2,1)}, u32[]{:S(2)}) copy-start(bf16[4,4,512]{1,0,2:T(4,128)(2,1)} %get-tuple-element.10) | copy-start | bytes 49156
  378.7 424.5 %all-reduce.5.cloned.1.call-start = ((), (), s32[]{:S(2)}) async-start(), calls=%async_computation.1 | async-start | bytes 262144 | tf_op jit(solution)/shard_map/psum | solution.py:128
  379.3 189.1 %copy-start.8 = (bf16[2048,32]{0,1:T(8,128)(2,1)S(1)}, bf16[2048,32]{0,1:T(8,128)(2,1)}, u32[]{:S(2)}) copy-start(bf16[2048,32]{0,1:T(8,128)(2,1)} %param.20) | copy-start | bytes 393220
  568.2 51.6 %copy-start.2 = (bf16[2048,128]{1,0:T(8,128)(2,1)S(1)}, bf16[2048,128]{1,0:T(8,128)(2,1)}, u32[]{:S(2)}) copy-start(bf16[2048,128]{1,0:T(8,128)(2,1)} %param.22) | copy-start | bytes 1572868
Sparse Core Ops, SparseCore 0:
  378.8 185.6 all-reduce.2
  621.0 182.0 all-reduce.4
where the time goes:
time: 812 us
  blocking collectives  394 us (49%)
  waiting for transfers between devices  368 us (45%)
  local copies, waits for them, and re-layouts  24.9 us (3%)
  between operations  13.7 us (2%)
    pmax x1, blocking collectives, shards(): overall = jnp.maximum(lax.pmax(cache_max, 'seq'), fresh_max)  243 us
    psum x1, waiting for transfers between devices, shards(): summed = lax.psum(packed, 'seq')  185 us
    psum x1, waiting for transfers between devices, shards(): down = lax.psum(down_part, 'seq')  182 us
    all_gather x1, blocking collectives, shards(): whole = lax.all_gather(picked, 'seq', axis=0, tiled=True)  51.6 us
    all_gather x1, blocking collectives, shards(): qkv_all = lax.all_gather(qkv_cols, 'seq', axis=2, tiled=True)  51.1 us
    all_gather x1, blocking collectives, shards(): projected = lax.all_gather(proj_cols, 'seq', axis=2, tiled=True)  48.3 us
  transfers between devices with their start and end apart: 2, of which 2 were waited for; matrix products, arithmetic and copies ran while one was open for 0% of the time, Pallas kernels for 0%

commit v1 on v0

--- a/solution.py
+++ b/solution.py
@@ -118,7 +118,9 @@
     proj_cols = jnp.einsum(
         "rsa,ac->rsc", attention, w_out, preferred_element_type=jnp.float32
     ).astype(jnp.bfloat16)
-    projected = lax.all_gather(proj_cols, "seq", axis=2, tiled=True)
+    projected = jnp.concatenate(
+        lax.all_to_all(jnp.stack([proj_cols] * lax.axis_size("seq")), "seq", 0, 0), axis=2
+    )
     middle = resid + branch_factor * projected.astype(jnp.float32)
     normed_mlp = rms_scale(middle, norm_mlp).astype(jnp.bfloat16)
     gate = jnp.einsum("rsd,df->rsf", normed_mlp, w_gate, preferred_element_type=jnp.float32)

time: 812 us -> 776 us (0.956)
  blocking collectives: 394 us -> 346 us
    all_gather x1 -> x0, blocking collectives: 48.3 us -> none  [shards(): projected = lax.all_gather(proj_cols, 'seq', axis=2, tiled=True)]
    all_to_all x0 -> x1, waiting for transfers between devices: none -> 9.72 us  [shards(): lax.all_to_all(jnp.stack([proj_cols] * lax.axis_size('seq')), 'seq', 0, 0)]
  transfers between devices with their start and end apart: 2 -> 3, of which waited for: 2 -> 3; matrix products, arithmetic and copies ran while one was open for 0% -> 0% of each run, Pallas kernels for 0% -> 0%
where the time goes in v1:
time: 776 us
  waiting for transfers between devices  375 us (48%)
  blocking collectives  346 us (45%)
  local copies, waits for them, and re-layouts  23.6 us (3%)
  between operations  13.7 us (2%)
    pmax x1, blocking collectives, shards(): overall = jnp.maximum(lax.pmax(cache_max, 'seq'), fresh_max)  243 us
    psum x1, waiting for transfers between devices, shards(): summed = lax.psum(packed, 'seq')  185 us
    psum x1, waiting for transfers between devices, shards(): down = lax.psum(down_part, 'seq')  180 us
    all_gather x1, blocking collectives, shards(): whole = lax.all_gather(picked, 'seq', axis=0, tiled=True)  51.6 us
    all_gather x1, blocking collectives, shards(): qkv_all = lax.all_gather(qkv_cols, 'seq', axis=2, tiled=True)  51.1 us
  transfers between devices with their start and end apart: 3, of which 3 were waited for; matrix products, arithmetic and copies ran while one was open for 0% of the time, Pallas kernels for 0%

profile of v1, /device:TPU:1, one launch (start us, length us, event | category | flops | bytes accessed | tf_op | source)
XLA Modules:
  0.0 775.8 jit_solution(17426872350603878344)
XLA Ops:
  6.5 0.8 reshape.196
  7.4 0.8 reshape.195
  8.2 6.4 copy.89
  14.6 4.2 gather_fusion
  18.9 51.6 %all-gather = bf16[64,32,16]{1,2,0:T(8,128)(2,1)S(1)} all-gather(bf16[1,32,16]{1,2,0:T(8,128)(2,1)S(1)} %select_bitcast_fusion), channel_id=1, replica_groups=mesh['seq'=64,'rep'=8] {'seq'}, dimensions={0}, use_global_device_ids=true | all-gather | bytes 66560 | tf_op jit(solution)/shard_map/all_gather | solution.py:73
  70.4 0.3 copy.90
  70.8 0.2 copy.91
  71.0 0.2 reshape.214
  71.5 0.2 convolution_convert_fusion.1
  71.7 0.1 copy.92
  71.9 51.1 %all_gather.7 = bf16[4,4,3072]{1,0,2:T(4,128)(2,1)S(1)} all-gather(bf16[4,4,48]{1,0,2:T(4,128)(2,1)S(1)} %copy.92), channel_id=1, replica_groups=mesh['seq'=64,'rep'=8] {'seq'}, dimensions={2}, use_global_device_ids=true | all-gather | bytes 99840 | tf_op jit(solution)/shard_map/all_gather | solution.py:85
  123.0 0.7 slice.38
  123.8 1.2 fusion.47
  124.9 1.3 copy.124
  126.2 0.2 reshape.202
  126.4 0.3 copy.125
  127.0 1.3 copy.96
  128.4 0.1 multiply_cosine_fusion
  128.5 0.1 subtract_convert_fusion
  128.7 0.2 pad_maximum_fusion.1
  128.9 0.4 select_reduce_fusion.1
  129.2 243.4 %pmax.7 = f32[4,4,8,4]{3,1,2,0:T(4,128)S(1)} all-reduce(f32[4,4,8,4]{3,1,2,0:T(4,128)S(1)} %get-tuple-element.19), channel_id=1, replica_groups=mesh['seq'=64,'rep'=8] {'seq'}, use_global_device_ids=true, to_apply=%region_2.3 | all-reduce | flops 512 | bytes 4096 | tf_op jit(solution)/shard_map/pmax | solution.py:108
  372.6 0.4 fusion.16
  373.1 0.3 copy.100
  373.4 1.3 select_reduce_fusion
  374.8 0.9 copy.102
  375.7 0.5 fusion.1
  376.1 0.9 pad_maximum_fusion
  377.1 0.4 fusion.18
  377.4 185.5 %all-reduce.3.cloned.1.call-done = f32[4,4,8,4,65]{4,3,1,2,0:T(4,128)} async-done(((f32[4,4,8,4,65]{4,3,1,2,0:T(4,128)}), f32[4,4,8,4,65]{4,3,1,2,0:T(4,128)}) %all-reduce.3.cloned.1.call-update) | async-done | bytes 133136 | tf_op jit(solution)/shard_map/psum | solution.py:113
  562.9 1.1 slice.46
  564.1 0.9 copy.123
  565.0 1.6 fusion.6
  566.6 0.1 reshape.200
  566.8 0.2 convolution_convert_fusion
  567.1 0.8 reshape.224
  567.9 6.5 all-to-all-start
  574.4 9.7 %all-to-all-done = bf16[64,2,256]{2,1,0:T(2,128)(2,1)S(1)} async-done(((bf16[64,2,256]{2,1,0:T(2,128)(2,1)}), bf16[64,2,256]{2,1,0:T(2,128)(2,1)S(1)}, u32[]{:S(2)}, u32[]{:S(2)}) %all-to-all-start) | async-done | bytes 65568 | tf_op jit(solution)/shard_map/all_to_all | solution.py:122
  584.1 0.2 reshape.225
  584.3 0.1 multiply_bitcast_fusion
  584.5 0.2 copy.109
  584.7 0.2 mul.259
  584.9 0.3 mul.258
  585.2 0.1 fusion.25
  585.5 1.2 fusion.12
  586.8 1.0 fusion.8
  587.8 179.5 %all-reduce.5.cloned.1.call-done = f32[4,4,2048]{2,1,0:T(4,128)} async-done(((f32[4,4,2048]{2,1,0:T(4,128)}), f32[4,4,2048]{2,1,0:T(4,128)}) %all-reduce.5.cloned.1.call-update) | async-done | bytes 131088 | tf_op jit(solution)/shard_map/psum | solution.py:130
  767.3 1.6 add_convert_fusion.1
  (47 shorter events, 1.3 us)
Async XLA Ops:
  6.5 580.2 %copy-start = (bf16[128,2048]{1,0:T(8,128)(2,1)S(1)}, bf16[128,2048]{1,0:T(8,128)(2,1)}, u32[]{:S(2)}) copy-start(bf16[128,2048]{1,0:T(8,128)(2,1)} %param.23) | copy-start | bytes 1572868
  6.5 556.4 %all-reduce.3.cloned.1.call-start = ((), (), s32[]{:S(2)}) async-start(), calls=%async_computation.1 | async-start | bytes 524288 | tf_op jit(solution)/shard_map/psum | solution.py:113
  8.1 63.3 %copy-start.4 = (bf16[2048]{0:T(1024)(128)(2,1)S(1)}, bf16[2048]{0:T(1024)(128)(2,1)}, u32[]{:S(2)}) copy-start(bf16[2048]{0:T(1024)(128)(2,1)} %param.17) | copy-start | bytes 12292
  8.1 63.3 %copy-start.7 = (bf16[2048,48]{0,1:T(8,128)(2,1)S(1)}, bf16[2048,48]{0,1:T(8,128)(2,1)}, u32[]{:S(2)}) copy-start(bf16[2048,48]{0,1:T(8,128)(2,1)} %param.19) | copy-start | bytes 589828
  123.8 2.6 copy-start.6
  126.2 246.9 %copy-start.1 = (bf16[4,128,512]{2,1,0:T(8,128)(2,1)S(1)}, bf16[4,128,512]{2,1,0:T(8,128)(2,1)}, u32[]{:S(2)}) copy-start(bf16[4,128,512]{2,1,0:T(8,128)(2,1)} %param.16) | copy-start | bytes 1572868
  375.7 189.3 %copy-start.3 = (bf16[4,4,512]{1,0,2:T(4,128)(2,1)S(1)}, bf16[4,4,512]{1,0,2:T(4,128)(2,1)}, u32[]{:S(2)}) copy-start(bf16[4,4,512]{1,0,2:T(4,128)(2,1)} %get-tuple-element.10) | copy-start | bytes 49156
  377.4 189.4 %copy-start.8 = (bf16[2048,32]{0,1:T(8,128)(2,1)S(1)}, bf16[2048,32]{0,1:T(8,128)(2,1)}, u32[]{:S(2)}) copy-start(bf16[2048,32]{0,1:T(8,128)(2,1)} %param.20) | copy-start | bytes 393220
  564.9 9.5 %copy-start.5 = (bf16[2048]{0:T(1024)(128)(2,1)S(1)}, bf16[2048]{0:T(1024)(128)(2,1)}, u32[]{:S(2)}) copy-start(bf16[2048]{0:T(1024)(128)(2,1)} %param.18) | copy-start | bytes 12292
  566.6 20.2 %copy-start.2 = (bf16[2048,128]{1,0:T(8,128)(2,1)S(1)}, bf16[2048,128]{1,0:T(8,128)(2,1)}, u32[]{:S(2)}) copy-start(bf16[2048,128]{1,0:T(8,128)(2,1)} %param.22) | copy-start | bytes 1572868
  567.9 16.2 %all-to-all-start = ((bf16[64,2,256]{2,1,0:T(2,128)(2,1)}), bf16[64,2,256]{2,1,0:T(2,128)(2,1)S(1)}, u32[]{:S(2)}, u32[]{:S(2)}) async-start(bf16[64,2,256]{2,1,0:T(2,128)(2,1)} %reshape.224), calls=%async_computation | async-start | bytes 131072 | tf_op jit(solution)/shard_map/all_to_all | solution.py:122
  574.4 193.0 %all-reduce.5.cloned.1.call-start = ((), (), s32[]{:S(2)}) async-start(), calls=%async_computation.2 | async-start | bytes 262144 | tf_op jit(solution)/shard_map/psum | solution.py:130
Sparse Core Ops, SparseCore 0:
  377.2 185.6 all-reduce.2
  587.9 179.3 all-reduce.4
